TPU v7x, 128 devices: a whole 4x4x4 slice. The times are simulated.
128 devices in a mesh: heads: 8 (over z, core), tok: 16 (over y, x).
Axes of the slice: x: 4, y: 4, z: 4, core: 2. Of those that a mesh axis runs over, the one named last changes fastest.
Arguments:
- states: bfloat16 [512, 7168], P('heads', 'tok'), may hold values from -10 to 10
- key_values: bfloat16 [2, 2, 8192, 7168], P(None, None, 'tok', 'heads')
- cache_length: int32 [2], replicated, may hold values from 0 to 7936, as said below
- norm1_gain: float32 [7168], replicated, may hold values from 0.25 to 1.75
- norm1_bias: float32 [7168], replicated, may hold values from -3 to 3
- qkv_weight: bfloat16 [7168, 3, 7168], P('tok', None, 'heads'), may hold values from -0.0625 to 0.0625
- qkv_bias: float32 [3, 7168], P(None, 'heads'), may hold values from -3 to 3
- out_weight: bfloat16 [7168, 7168], P('heads', 'tok'), may hold values from -0.0625 to 0.0625
- out_bias: float32 [7168], P('tok'), may hold values from -3 to 3
- norm2_gain: float32 [7168], replicated, may hold values from 0.25 to 1.75
- norm2_bias: float32 [7168], replicated, may hold values from -3 to 3
- fc1_weight: bfloat16 [7168, 28672], P(None, ('heads', 'tok')), may hold values from -0.0625 to 0.0625
- fc1_bias: float32 [28672], P(('heads', 'tok')), may hold values from -3 to 3
- fc2_weight: bfloat16 [28672, 7168], P(('heads', 'tok')), may hold values from -0.03125 to 0.03125
- fc2_bias: float32 [7168], P('tok'), may hold values from -3 to 3
Outputs:
- hidden_out: bfloat16 [512, 7168], P('heads', 'tok')
- cache_out: bfloat16 [2, 2, 8192, 7168], P(None, None, 'tok', 'heads')
Inputs may be any that keep to these rules, and one draw needn't show every extreme that they name: Request r's new tokens take positions cache_length[r] to cache_length[r] + 255 of its cache; some request reaches the largest length.
All inputs are finite; a program needn't handle non-finite values.
Results may differ from a plain program's by a relative error of at most 0.013.
The roundings to bfloat16 on the way count: a program that leaves them out, or rounds other values in their place, can miss the bound.
Values may be sent and summed in bfloat16 or wider, within the bound.
A program may use at most 192 MiB of HBM per device.

v0:
```python
import jax
import jax.numpy as jnp
from jax import lax
from jax.sharding import PartitionSpec as P

HD = 128
SINK = 4
REQS = 2
NEW = 256
EPSILON = 1e-05
NEGATIVE = -1e30


def joined(value, axis, join):
    pieces = jax.tree.map(lambda part: lax.all_gather(part, axis), value)
    head = jax.tree.map(lambda part: part[0], pieces)
    tail = jax.tree.map(lambda part: part[1:], pieces)
    so_far, _ = lax.scan(lambda so_far, section: (join(so_far, section), None), head, tail)
    return so_far


def norm_rows(values, total_sum, total_square, width, gain, shift):
    mean_row = total_sum / width
    variance = total_square / width - mean_row * mean_row
    return (
        (values - mean_row[:, None]) * lax.rsqrt(variance[:, None] + EPSILON) * gain + shift
    ).astype(jnp.bfloat16)


def merge_parts(first, second):
    highest = jnp.maximum(first[1], second[1])
    left_factor = jnp.exp(first[1] - highest)
    right_factor = jnp.exp(second[1] - highest)
    return (
        first[0] * left_factor[..., None] + second[0] * right_factor[..., None],
        highest,
        first[2] * left_factor + second[2] * right_factor,
    )


def shards(
    states,
    key_values,
    cache_length,
    norm1_gain,
    norm1_bias,
    qkv_weight,
    qkv_bias,
    out_weight,
    out_bias,
    norm2_gain,
    norm2_bias,
    fc1_weight,
    fc1_bias,
    fc2_weight,
    fc2_bias,
):
    head_count = lax.axis_size("heads")
    tok_count = lax.axis_size("tok")
    tok_index = lax.axis_index("tok")
    rows_local, cols_local = states.shape
    width = cols_local * tok_count
    group = qkv_weight.shape[2]
    group_heads = group // HD
    tokens = rows_local * head_count
    cache_rows = key_values.shape[2]
    window = cache_rows * tok_count // 2
    col_start = tok_index * cols_local
    states_float = states.astype(jnp.float32)
    row_sum, row_square = lax.psum(
        (jnp.sum(states_float, axis=1), jnp.sum(states_float * states_float, axis=1)), "tok"
    )
    gain_one = lax.dynamic_slice_in_dim(norm1_gain, col_start, cols_local)
    shift_one = lax.dynamic_slice_in_dim(norm1_bias, col_start, cols_local)
    normed_one = norm_rows(states_float, row_sum, row_square, width, gain_one, shift_one)
    gathered = lax.all_gather(normed_one, "heads", axis=0, tiled=True)
    weight_flat = qkv_weight.reshape(cols_local, 3 * group)
    factors = jnp.asarray([HD ** (-0.5), 1.0, 1.0], dtype=jnp.float32)[None, :, None]
    partial_qkv = jnp.dot(gathered, weight_flat, preferred_element_type=jnp.float32)
    summed = lax.psum(partial_qkv, "tok")
    projected = ((summed.reshape(tokens, 3, group) + qkv_bias[None]) * factors).astype(jnp.bfloat16)
    queries = projected[:, 0].reshape(REQS, NEW, group_heads, HD)
    fresh = jnp.moveaxis(projected[:, 1:].reshape(REQS, NEW, 2, group), 2, 0)
    key_pos = tok_index * cache_rows + jnp.arange(cache_rows, dtype=jnp.int32)
    appended_parts = []
    for request in range(REQS):
        offset = key_pos - cache_length[request]
        inside = (offset >= 0) & (offset < NEW)
        picked = jnp.take(fresh[:, request], jnp.clip(offset, 0, NEW - 1), axis=1)
        appended_parts.append(jnp.where(inside[None, :, None], picked, key_values[:, request]))
    appended = jnp.stack(appended_parts, axis=1)
    keys = appended[0].reshape(REQS, cache_rows, group_heads, HD)
    values = appended[1].reshape(REQS, cache_rows, group_heads, HD)
    query_pos = cache_length[:, None] + jnp.arange(NEW, dtype=jnp.int32)[None, :]
    distance = query_pos[:, :, None] - key_pos[None, None, :]
    allowed = (distance >= 0) & ((key_pos[None, None, :] < SINK) | (distance < window))
    scores = jnp.einsum("rshd,rphd->rshp", queries, keys, preferred_element_type=jnp.float32)
    masked = jnp.where(allowed[:, :, None, :], scores, NEGATIVE)
    peak = jnp.max(masked, axis=-1)
    weights = jnp.where(allowed[:, :, None, :], jnp.exp(masked - peak[..., None]), 0.0)
    totals = jnp.sum(weights, axis=-1)
    partial_out = jnp.einsum(
        "rshp,rphd->rshd", weights.astype(jnp.bfloat16), values, preferred_element_type=jnp.float32
    )
    merged, highest, denominator = joined((partial_out, peak, totals), "tok", merge_parts)
    attended = (merged / denominator[..., None]).astype(jnp.bfloat16).reshape(tokens, group)
    projected_out = lax.psum_scatter(
        jnp.dot(attended, out_weight, preferred_element_type=jnp.float32),
        "heads",
        scatter_dimension=0,
        tiled=True,
    )
    residual = (states_float + projected_out + out_bias).astype(jnp.bfloat16)
    residual_float = residual.astype(jnp.float32)
    second_sum, second_square = lax.psum(
        (jnp.sum(residual_float, axis=1), jnp.sum(residual_float * residual_float, axis=1)), "tok"
    )
    gain_two = lax.dynamic_slice_in_dim(norm2_gain, col_start, cols_local)
    shift_two = lax.dynamic_slice_in_dim(norm2_bias, col_start, cols_local)
    normed_part = norm_rows(residual_float, second_sum, second_square, width, gain_two, shift_two)
    normed = lax.all_gather(normed_part, "tok", axis=1, tiled=True)
    active = jnp.maximum(
        jnp.dot(
            lax.all_gather(normed, "heads", axis=0, tiled=True),
            fc1_weight,
            preferred_element_type=jnp.float32,
        )
        + fc1_bias,
        0.0,
    ).astype(jnp.bfloat16)
    hidden_local = fc1_weight.shape[1]
    term = jnp.einsum(
        "hnf,ftc->htnc",
        active.reshape(head_count, rows_local, hidden_local),
        fc2_weight.reshape(hidden_local, tok_count, cols_local),
        preferred_element_type=jnp.float32,
    )
    down = lax.psum_scatter(
        term.reshape(head_count * tok_count * rows_local, cols_local),
        ("heads", "tok"),
        scatter_dimension=0,
        tiled=True,
    )
    hidden_out = (residual_float + down + fc2_bias).astype(jnp.bfloat16)
    return (hidden_out, appended)


def solution(mesh):
    placed = (
        P("heads", "tok"),
        P(None, None, "tok", "heads"),
        P(),
        P(),
        P(),
        P("tok", None, "heads"),
        P(None, "heads"),
        P("heads", "tok"),
        P("tok"),
        P(),
        P(),
        P(None, ("heads", "tok")),
        P(("heads", "tok")),
        P(("heads", "tok"), None),
        P("tok"),
    )
    return jax.shard_map(
        shards,
        mesh=mesh,
        in_specs=placed,
        out_specs=(P("heads", "tok"), P(None, None, "tok", "heads")),
        check_vma=False,
    )
```

profile of v0, /device:TPU:0, one launch (start us, length us, event | category | flops | bytes accessed | tf_op | source)
XLA Modules:
  0.0 1517.9 jit_solution(4574828928947439626)
XLA Ops:
  9.9 40.7 %all-reduce.1 = (f32[64]{0:T(128)S(1)}, f32[64]{0:T(128)S(1)}) all-reduce(f32[64]{0:T(128)S(1)} %get-tuple-element.71, f32[64]{0:T(128)S(1)} %get-tuple-element.70), channel_id=1, replica_groups=mesh['heads'=8,'tok'=16] {'tok'}, use_global_device_ids=true, to_apply=%region_3.0 | all-reduce | flops 128 | bytes 1024 | tf_op jit(solution)/shard_map/psum | solution.py:70
  51.6 15.4 %all_gather.27 = bf16[512,448]{1,0:T(8,128)(2,1)} all-gather(bf16[64,448]{1,0:T(8,128)(2,1)S(1)} %fusion.33), channel_id=1, replica_groups=mesh['heads'=8,'tok'=16] {'heads'}, dimensions={0}, use_global_device_ids=true | all-gather | bytes 516096 | tf_op jit(solution)/shard_map/all_gather | solution.py:76
  87.2 101.3 %all-reduce.4.cloned.1.call-done = f32[512,3,896]{0,2,1:T(8,128)} async-done(((f32[512,3,896]{0,2,1:T(8,128)}), f32[512,3,896]{0,2,1:T(8,128)}) %all-reduce.4.cloned.1.call-update) | async-done | bytes 5505040 | tf_op jit(solution)/shard_map/psum | solution.py:80
  194.0 6.1 copy.47
  204.1 6.9 gather_fusion
  211.0 6.8 gather_fusion.1
  217.8 17.6 %fusion.16 = (bf16[2,1,512,896]{3,0,2,1:T(2,128)(2,1)S(1)}, bf16[2,1,512,896]{3,0,2,1:T(2,128)(2,1)S(1)}) fusion(bf16[2,1,512,896]{3,2,1,0:T(8,128)(2,1)} %get-tuple-element.99, bf16[512,2,896]{2,1,0:T(2,128)(2,1)} %gather_fusion, pred[512]{0:T(512)(128)(4,1)S(1)} %compare_and_fusion.1, pred[512]{0:T(512)(128)(4,1)S(1)} %fusion.53, ...), kind=kLoop, calls=%fused_computation.38 | loop fusion | flops 3670016 | bytes 11012096 | tf_op jit(solution)/shard_map/stack | solution.py:91
  235.4 11.7 slice_maximum_fusion
  247.1 9.3 copy.50
  256.4 9.3 copy.51
  280.8 23.8 %all-gather.1 = f32[32,256,7]{1,2,0:T(8,128)S(1)} all-gather(f32[2,256,7]{1,2,0:T(8,128)S(1)} %get-tuple-element.109), channel_id=3, replica_groups=mesh['heads'=8,'tok'=16] {'tok'}, dimensions={0}, use_global_device_ids=true | all-gather | bytes 243712 | tf_op jit(solution)/shard_map/all_gather | solution.py:15
  310.0 22.1 %all-gather.2 = f32[32,256,7]{1,2,0:T(8,128)S(1)} all-gather(f32[2,256,7]{1,2,0:T(8,128)S(1)} %fusion.5), channel_id=4, replica_groups=mesh['heads'=8,'tok'=16] {'tok'}, dimensions={0}, use_global_device_ids=true | all-gather | bytes 243712 | tf_op jit(solution)/shard_map/all_gather | solution.py:15
  333.9 124.0 %all-gather.9.cloned.1.call-done = f32[32,256,7,128]{3,1,2,0:T(8,128)} async-done(((f32[2,256,7,128]{3,1,2,0:T(8,128)}), f32[32,256,7,128]{3,1,2,0:T(8,128)}) %all-gather.9.cloned.1.call-update) | async-done | bytes 29360144 | tf_op jit(solution)/shard_map/all_gather | solution.py:15
  461.8 20.8 %slice.86 = f32[30,256,7,128]{3,1,2,0:T(8,128)} slice(f32[32,256,7,128]{3,1,2,0:T(8,128)} %all-gather.9.cloned.1.call-done), slice={[2:32], [0:256], [0:7], [0:128]} | slice | bytes 55050240 | tf_op jit(solution)/shard_map/slice | solution.py:17
  482.6 185.3 %while.14 = (s32[]{:T(128)}, f32[2,256,7,128]{3,2,1,0:T(8,128)}, f32[2,256,7]{2,1,0:T(8,128)}, f32[2,256,7]{2,1,0:T(8,128)}, f32[15,2,256,7]{2,3,1,0:T(8,128)}, ...) while((s32[]{:T(128)}, f32[2,256,7,128]{3,2,1,0:T(8,128)}, ...), condition=%wide.region_8.10_spmd, body=%wide.region_7.9_spmd.sunk | while | flops 1397762 | bytes 18493624 | solution.py:18
  673.3 30.4 %reduce-scatter.3.cloned.1.call-done = f32[64,448]{1,0:T(8,128)} async-done(((f32[512,448]{1,0:T(8,128)}), f32[64,448]{1,0:T(8,128)}) %reduce-scatter.3.cloned.1.call-update) | async-done | bytes 114704 | tf_op jit(solution)/shard_map/reduce_scatter | solution.py:107
  704.8 40.2 %all-reduce = (f32[64]{0:T(128)S(1)}, f32[64]{0:T(128)S(1)}) all-reduce(f32[64]{0:T(128)S(1)} %get-tuple-element.69, f32[64]{0:T(128)S(1)} %get-tuple-element.68), channel_id=1, replica_groups=mesh['heads'=8,'tok'=16] {'tok'}, use_global_device_ids=true, to_apply=%region_13.15 | all-reduce | flops 128 | bytes 1024 | tf_op jit(solution)/shard_map/psum | solution.py:115
  745.1 21.6 %all-gather.3 = bf16[16,448,64]{1,2,0:T(8,128)(2,1)S(1)} all-gather(bf16[1,448,64]{1,2,0:T(8,128)(2,1)S(1)} %fusion.44), channel_id=1, replica_groups=mesh['heads'=8,'tok'=16] {'tok'}, dimensions={0}, use_global_device_ids=true | all-gather | bytes 974848 | tf_op jit(solution)/shard_map/all_gather | solution.py:121
  771.3 7.5 reshape.104
  778.8 35.7 %all-gather.7.cloned.1.call-done = bf16[512,7168]{1,0:T(8,128)(2,1)} async-done(((bf16[64,7168]{1,0:T(8,128)(2,1)}), bf16[512,7168]{1,0:T(8,128)(2,1)}) %all-gather.7.cloned.1.call-update) | async-done | bytes 7340048 | tf_op jit(solution)/shard_map/all_gather | solution.py:124
  814.5 6.1 fusion.22
  821.7 13.0 fusion.9
  834.7 7.6 pad_maximum_fusion
  844.6 665.0 %reduce-scatter.5.cloned.1.call-done = f32[64,448]{1,0:T(8,128)} async-done(((f32[8192,448]{1,0:T(8,128)}), f32[64,448]{1,0:T(8,128)}) %reduce-scatter.5.cloned.1.call-update) | async-done | bytes 114704 | tf_op jit(solution)/shard_map/reduce_scatter | solution.py:138
  (267 shorter events, 260.6 us)
Async XLA Ops:
  7.2 807.3 %copy-start = (bf16[7168,224]{0,1:T(8,128)(2,1)S(1)}, bf16[7168,224]{0,1:T(8,128)(2,1)}, u32[]{:S(2)}) copy-start(bf16[7168,224]{0,1:T(8,128)(2,1)} %param.31) | copy-start | bytes 9633796
  7.2 181.4 %all-reduce.4.cloned.1.call-start = ((), (), s32[]{:S(2)}) async-start(), calls=%async_computation.2 | async-start | bytes 11010048 | tf_op jit(solution)/shard_map/psum | solution.py:80
  77.3 380.6 %all-gather.9.cloned.1.call-start = ((), (), s32[]{:S(2)}) async-start(), calls=%async_computation.6 | async-start | bytes 31195136 | tf_op jit(solution)/shard_map/all_gather | solution.py:15
  82.9 105.6 %copy-start.9 = (f32[3,896]{1,0:T(4,128)S(1)}, f32[3,896]{1,0:T(4,128)}, u32[]{:S(2)}) copy-start(f32[3,896]{1,0:T(4,128)} %param.26) | copy-start | bytes 32260
  83.0 105.6 %copy-start.13 = (f32[3]{0:T(128)S(1)}, f32[3]{0:T(128)}, u32[]{:S(2)}) copy-start(f32[3]{0:T(128)} %constant.59.clone) | copy-start | bytes 40
  235.4 11.7 copy-start.3
  235.4 11.7 copy-start.4
  268.8 6.2 copy-start.5
  280.8 422.9 %reduce-scatter.3.cloned.1.call-start = ((), (), s32[]{:S(2)}) async-start(), calls=%async_computation.3 | async-start | bytes 1179648 | tf_op jit(solution)/shard_map/reduce_scatter | solution.py:107
  501.9 5.4 copy-start.8
  514.3 5.4 copy-start.8
  539.0 5.4 copy-start.8
  551.3 5.4 copy-start.8
  563.7 5.4 copy-start.8
  588.4 5.4 copy-start.8
  600.7 5.4 copy-start.8
  613.1 5.4 copy-start.8
  637.8 5.4 copy-start.8
  670.0 33.8 %copy-start.6 = (bf16[64,448]{1,0:T(8,128)(2,1)S(1)}, bf16[64,448]{1,0:T(8,128)(2,1)}, u32[]{:S(2)}) copy-start(bf16[64,448]{1,0:T(8,128)(2,1)} %param.20) | copy-start | bytes 172036
  670.0 33.8 %copy-start.11 = (f32[448]{0:T(512)S(1)}, f32[448]{0:T(512)}, u32[]{:S(2)}) copy-start(f32[448]{0:T(512)} %param.28) | copy-start | bytes 5380
  671.7 142.8 %all-gather.7.cloned.1.call-start = ((), (), s32[]{:S(2)}) async-start(), calls=%async_computation.4 | async-start | bytes 8257536 | tf_op jit(solution)/shard_map/all_gather | solution.py:124
  771.2 43.2 %copy-start.15 = (f32[224]{0:T(256)S(1)}, f32[224]{0:T(256)}, u32[]{:S(2)}) copy-start(f32[224]{0:T(256)} %param.32) | copy-start | bytes 2692
  771.3 738.4 %reduce-scatter.5.cloned.1.call-start = ((), (), s32[]{:S(2)}) async-start(), calls=%async_computation.5 | async-start | bytes 16908288 | tf_op jit(solution)/shard_map/reduce_scatter | solution.py:138
  842.3 667.3 %copy-start.12 = (f32[448]{0:T(512)S(1)}, f32[448]{0:T(512)}, u32[]{:S(2)}) copy-start(f32[448]{0:T(512)} %param.34) | copy-start | bytes 5380
  (40 other events, 127.9 us)
Sparse Core Ops, SparseCore 0:
  77.5 111.0 all-reduce.3
  280.9 176.9 all-gather.8
  671.8 31.8 reduce-scatter.2
  771.4 43.0 all-gather.6
  834.8 674.7 reduce-scatter.4
where the time goes:
time: 1530 us; the launch traced here: 1520 us
  waiting for transfers between devices  957 us (63%)
  local copies, waits for them, and re-layouts  181 us (12%)
  other arithmetic  169 us (11%)
  blocking collectives  164 us (11%)
  matrix products  33 us (2%)
    reduce_scatter x1, waiting for transfers between devices, shards(): lax.psum_scatter(term.reshape(head_count * tok_count * rows_local, cols_l...  665 us
    all_gather x1, waiting for transfers between devices, joined(): pieces = jax.tree.map(lambda part: lax.all_gather(part, axis), value)  124 us
    psum x1, waiting for transfers between devices, shards(): summed = lax.psum(partial_qkv, 'tok')  101 us
    add x15, other arithmetic, merge_parts(): first[0] * left_factor[..., None] + second[0] * right_factor[..., None]  81.5 us
    dynamic_slice x60, local copies, waits for them, and re-layouts, joined(): lax.scan(lambda so_far, section: (join(so_far, section), None), head, tail)  71.5 us
    all_gather x2, blocking collectives, joined(): pieces = jax.tree.map(lambda part: lax.all_gather(part, axis), value)  45.8 us
    psum x1, blocking collectives, shards(): lax.psum((jnp.sum(states_float, axis=1), jnp.sum(states_float * states_fl...  40.7 us
    psum x1, blocking collectives, shards(): lax.psum((jnp.sum(residual_float, axis=1), jnp.sum(residual_float * resid...  40.2 us
  transfers between devices with their start and end apart: 5, of which 5 were waited for; matrix products, arithmetic and copies ran while one was open for 2% of the time, Pallas kernels for 0%

commit v1 on v0

--- a/solution.py
+++ b/solution.py
@@ -9,6 +9,12 @@
 NEW = 256
 EPSILON = 1e-05
 NEGATIVE = -1e30
+
+
+def gather_and_add(block, mesh_axis):
+    parts = lax.all_gather(block, mesh_axis, axis=0, tiled=False)
+    total = parts.sum(axis=0)
+    return total
 
 
 def joined(value, axis, join):
@@ -77,7 +83,7 @@
     weight_flat = qkv_weight.reshape(cols_local, 3 * group)
     factors = jnp.asarray([HD ** (-0.5), 1.0, 1.0], dtype=jnp.float32)[None, :, None]
     partial_qkv = jnp.dot(gathered, weight_flat, preferred_element_type=jnp.float32)
-    summed = lax.psum(partial_qkv, "tok")
+    summed = gather_and_add(partial_qkv, "tok")
     projected = ((summed.reshape(tokens, 3, group) + qkv_bias[None]) * factors).astype(jnp.bfloat16)
     queries = projected[:, 0].reshape(REQS, NEW, group_heads, HD)
     fresh = jnp.moveaxis(projected[:, 1:].reshape(REQS, NEW, 2, group), 2, 0)

time: 1530 us -> 1860 us (1.22)
  waiting for transfers between devices: 957 us -> 1320 us
  other arithmetic: 169 us -> 142 us
    all_gather x0 -> x1, waiting for transfers between devices: none -> 460 us  [gather_and_add(): parts = lax.all_gather(block, mesh_axis, axis=0, tiled=False)]
    psum x1 -> x0, waiting for transfers between devices: 101 us -> none  [shards(): summed = lax.psum(partial_qkv, 'tok')]
    add x15, other arithmetic: 81.5 us -> 24.5 us  [merge_parts(): first[0] * left_factor[..., None] + second[0] * right_factor[..., None]]
    reduce_sum x0 -> x1, other arithmetic: none -> 30.1 us  [gather_and_add(): total = parts.sum(axis=0)]
    dynamic_slice x60, local copies, waits for them, and re-layouts: 71.5 us -> 50.2 us  [joined(): lax.scan(lambda so_far, section: (join(so_far, section), None), head, tail)]
    while x90 -> x120, local copies, waits for them, and re-layouts: 0.17 us -> 19.9 us
where the time goes in v1:
time: 1860 us
  waiting for transfers between devices  1320 us (71%)
  local copies, waits for them, and re-layouts  186 us (10%)
  blocking collectives  164 us (9%)
  other arithmetic  142 us (8%)
  matrix products  33.1 us (2%)
    reduce_scatter x1, waiting for transfers between devices, shards(): lax.psum_scatter(term.reshape(head_count * tok_count * rows_local, cols_l...  665 us
    all_gather x1, waiting for transfers between devices, gather_and_add(): parts = lax.all_gather(block, mesh_axis, axis=0, tiled=False)  460 us
    all_gather x1, waiting for transfers between devices, joined(): pieces = jax.tree.map(lambda part: lax.all_gather(part, axis), value)  124 us
    dynamic_slice x60, local copies, waits for them, and re-layouts, joined(): lax.scan(lambda so_far, section: (join(so_far, section), None), head, tail)  50.2 us
    all_gather x2, blocking collectives, joined(): pieces = jax.tree.map(lambda part: lax.all_gather(part, axis), value)  46.1 us
    psum x1, blocking collectives, shards(): lax.psum((jnp.sum(states_float, axis=1), jnp.sum(states_float * states_fl...  40.7 us
    psum x1, blocking collectives, shards(): lax.psum((jnp.sum(residual_float, axis=1), jnp.sum(residual_float * resid...  40.2 us
  transfers between devices with their start and end apart: 5, of which 5 were waited for; matrix products, arithmetic and copies ran while one was open for 2% of the time, Pallas kernels for 0%

profile of v1, /device:TPU:0, one launch (start us, length us, event | category | flops | bytes accessed | tf_op | source)
XLA Modules:
  0.0 1856.8 jit_solution(4599868131708025216)
XLA Ops:
  9.9 40.7 %all-reduce.1 = (f32[64]{0:T(128)S(1)}, f32[64]{0:T(128)S(1)}) all-reduce(f32[64]{0:T(128)S(1)} %get-tuple-element.71, f32[64]{0:T(128)S(1)} %get-tuple-element.70), channel_id=1, replica_groups=mesh['heads'=8,'tok'=16] {'tok'}, use_global_device_ids=true, to_apply=%region_3.0 | all-reduce | flops 128 | bytes 1024 | tf_op jit(solution)/shard_map/psum | solution.py:76
  51.6 15.4 all_gather.33
  88.7 460.2 %all-gather.11.cloned.1.call-done = f32[8192,2688]{1,0:T(8,128)} async-done(((f32[512,2688]{1,0:T(8,128)}), f32[8192,2688]{1,0:T(8,128)}) %all-gather.11.cloned.1.call-update) | async-done | bytes 88080400 | tf_op jit(solution)/shard_map/all_gather | solution.py:15
  548.9 30.1 %reduce_sum.56 = f32[512,2688]{1,0:T(8,128)} reduce(f32[16,512,2688]{2,1,0:T(8,128)} %bitcast.5, f32[]{:T(128)} %constant.14.clone.1), dimensions={0}, to_apply=%region_4.0 | reduce | flops 20643840 | bytes 93585408 | tf_op jit(solution)/shard_map/reduce_sum | solution.py:16
  579.0 6.2 copy.45
  600.2 6.8 gather_fusion
  607.1 6.8 gather_fusion.1
  613.9 17.7 fusion.16
  631.7 11.5 slice_maximum_fusion
  643.2 9.3 copy.50
  655.7 9.3 copy.49
  681.6 23.9 %all-gather.3 = f32[32,256,7]{1,2,0:T(8,128)S(1)} all-gather(f32[2,256,7]{1,2,0:T(8,128)S(1)} %fusion.5), channel_id=5, replica_groups=mesh['heads'=8,'tok'=16] {'tok'}, dimensions={0}, use_global_device_ids=true | all-gather | bytes 243712 | tf_op jit(solution)/shard_map/all_gather | solution.py:21
  705.5 22.2 %all-gather.2 = f32[32,256,7]{1,2,0:T(8,128)S(1)} all-gather(f32[2,256,7]{1,2,0:T(8,128)S(1)} %get-tuple-element.109), channel_id=4, replica_groups=mesh['heads'=8,'tok'=16] {'tok'}, dimensions={0}, use_global_device_ids=true | all-gather | bytes 243712 | tf_op jit(solution)/shard_map/all_gather | solution.py:21
  730.2 124.4 %all-gather.13.cloned.1.call-done = f32[32,256,7,128]{3,1,2,0:T(8,128)} async-done(((f32[2,256,7,128]{3,1,2,0:T(8,128)}), f32[32,256,7,128]{3,1,2,0:T(8,128)}) %all-gather.13.cloned.1.call-update) | async-done | bytes 29360144 | tf_op jit(solution)/shard_map/all_gather | solution.py:21
  858.5 20.9 %slice.86 = f32[30,256,7,128]{3,1,2,0:T(8,128)} slice(f32[32,256,7,128]{3,1,2,0:T(8,128)} %all-gather.13.cloned.1.call-done), slice={[2:32], [0:256], [0:7], [0:128]} | slice | bytes 55050240 | tf_op jit(solution)/shard_map/slice | solution.py:23
  879.3 127.5 %while.14 = (s32[]{:T(128)}, f32[2,256,7,128]{3,2,1,0:T(8,128)}, f32[2,256,7]{2,1,0:T(8,128)}, f32[2,256,7]{2,1,0:T(8,128)}, f32[15,2,256,7]{2,3,1,0:T(8,128)}, ...) while((s32[]{:T(128)}, f32[2,256,7,128]{3,2,1,0:T(8,128)}, ...), condition=%wide.region_8.10_spmd, body=%wide.region_7.9_spmd.sunk | while | flops 1397762 | bytes 25833676 | solution.py:24
  1012.3 30.4 %reduce-scatter.3.cloned.1.call-done = f32[64,448]{1,0:T(8,128)} async-done(((f32[512,448]{1,0:T(8,128)}), f32[64,448]{1,0:T(8,128)}) %reduce-scatter.3.cloned.1.call-update) | async-done | bytes 114704 | tf_op jit(solution)/shard_map/reduce_scatter | solution.py:113
  1043.7 40.2 %all-reduce = (f32[64]{0:T(128)S(1)}, f32[64]{0:T(128)S(1)}) all-reduce(f32[64]{0:T(128)S(1)} %get-tuple-element.69, f32[64]{0:T(128)S(1)} %get-tuple-element.68), channel_id=1, replica_groups=mesh['heads'=8,'tok'=16] {'tok'}, use_global_device_ids=true, to_apply=%region_13.15 | all-reduce | flops 128 | bytes 1024 | tf_op jit(solution)/shard_map/psum | solution.py:121
  1084.1 21.6 %all-gather.4 = bf16[16,448,64]{1,2,0:T(8,128)(2,1)S(1)} all-gather(bf16[1,448,64]{1,2,0:T(8,128)(2,1)S(1)} %fusion.44), channel_id=1, replica_groups=mesh['heads'=8,'tok'=16] {'tok'}, dimensions={0}, use_global_device_ids=true | all-gather | bytes 974848 | tf_op jit(solution)/shard_map/all_gather | solution.py:127
  1110.3 7.5 reshape.104
  1117.7 35.7 %all-gather.9.cloned.1.call-done = bf16[512,7168]{1,0:T(8,128)(2,1)} async-done(((bf16[64,7168]{1,0:T(8,128)(2,1)}), bf16[512,7168]{1,0:T(8,128)(2,1)}) %all-gather.9.cloned.1.call-update) | async-done | bytes 7340048 | tf_op jit(solution)/shard_map/all_gather | solution.py:130
  1160.7 13.0 fusion.9
  1173.7 7.6 pad_maximum_fusion
  1183.6 664.9 %reduce-scatter.5.cloned.1.call-done = f32[64,448]{1,0:T(8,128)} async-done(((f32[8192,448]{1,0:T(8,128)}), f32[64,448]{1,0:T(8,128)}) %reduce-scatter.5.cloned.1.call-update) | async-done | bytes 114704 | tf_op jit(solution)/shard_map/reduce_scatter | solution.py:144
  (299 shorter events, 215.3 us)
Async XLA Ops:
  7.2 1146.3 %copy-start = (bf16[7168,224]{0,1:T(8,128)(2,1)S(1)}, bf16[7168,224]{0,1:T(8,128)(2,1)}, u32[]{:S(2)}) copy-start(bf16[7168,224]{0,1:T(8,128)(2,1)} %param.31) | copy-start | bytes 9633796
  7.2 541.7 %all-gather.11.cloned.1.call-start = ((), (), s32[]{:S(2)}) async-start(), calls=%async_computation.5 | async-start | bytes 93585408 | tf_op jit(solution)/shard_map/all_gather | solution.py:15
  77.4 777.2 %all-gather.13.cloned.1.call-start = ((), (), s32[]{:S(2)}) async-start(), calls=%async_computation.6 | async-start | bytes 31195136 | tf_op jit(solution)/shard_map/all_gather | solution.py:21
  579.0 6.2 copy-start.10
  579.0 6.2 copy-start.14
  631.6 11.5 copy-start.4
  631.7 11.5 copy-start.5
  665.0 6.2 copy-start.6
  676.9 365.8 %reduce-scatter.3.cloned.1.call-start = ((), (), s32[]{:S(2)}) async-start(), calls=%async_computation.2 | async-start | bytes 1179648 | tf_op jit(solution)/shard_map/reduce_scatter | solution.py:113
  881.1 3.8 copy-start.1
  889.6 3.8 copy-start.1
  898.1 3.8 copy-start.1
  906.6 3.8 copy-start.1
  915.1 3.8 copy-start.1
  932.1 3.8 copy-start.1
  957.6 3.8 copy-start.1
  966.1 3.8 copy-start.1
  991.6 3.8 copy-start.1
  1008.9 33.8 %copy-start.7 = (bf16[64,448]{1,0:T(8,128)(2,1)S(1)}, bf16[64,448]{1,0:T(8,128)(2,1)}, u32[]{:S(2)}) copy-start(bf16[64,448]{1,0:T(8,128)(2,1)} %param.20) | copy-start | bytes 172036
  1008.9 33.8 %copy-start.12 = (f32[448]{0:T(512)S(1)}, f32[448]{0:T(512)}, u32[]{:S(2)}) copy-start(f32[448]{0:T(512)} %param.28) | copy-start | bytes 5380
  1010.7 142.8 %all-gather.9.cloned.1.call-start = ((), (), s32[]{:S(2)}) async-start(), calls=%async_computation.3 | async-start | bytes 8257536 | tf_op jit(solution)/shard_map/all_gather | solution.py:130
  1110.2 43.2 %copy-start.16 = (f32[224]{0:T(256)S(1)}, f32[224]{0:T(256)}, u32[]{:S(2)}) copy-start(f32[224]{0:T(256)} %param.32) | copy-start | bytes 2692
  1110.2 738.2 %reduce-scatter.5.cloned.1.call-start = ((), (), s32[]{:S(2)}) async-start(), calls=%async_computation.4 | async-start | bytes 16908288 | tf_op jit(solution)/shard_map/reduce_scatter | solution.py:144
  1181.3 667.2 %copy-start.13 = (f32[448]{0:T(512)S(1)}, f32[448]{0:T(512)}, u32[]{:S(2)}) copy-start(f32[448]{0:T(512)} %param.34) | copy-start | bytes 5380
  (55 other events, 105.2 us)
Sparse Core Ops, SparseCore 0:
  77.5 471.2 all-gather.10
  677.1 177.4 all-gather.12
  1010.8 31.8 reduce-scatter.2
  1110.3 43.0 all-gather.8
  1173.8 674.5 reduce-scatter.4
